TPU v7x, 256 devices: a whole 4x4x8 slice. The times are simulated.
256 devices in a mesh: ctx: 32 (over x, z_hi, y), exp: 8 (over z_lo, core).
Axes of the slice: x: 4, y: 4, z: 8 (z_hi: 2, z_lo: 4; z = z_hi * 4 + z_lo), core: 2. Of those that a mesh axis runs over, the one named last changes fastest.
Arguments:
- queries: bfloat16 [256, 32, 128], P(None, 'exp'), may hold values from -64 to 64
- keys: bfloat16 [32768, 8, 128], P('ctx', 'exp'), may hold values from -8 to 8
- values: bfloat16 [32768, 8, 128], P('ctx', 'exp'), may hold values from -32 to 32
- out_proj: bfloat16 [4096, 4096], P('exp', 'ctx'), may hold values from -0.09375 to 0.09375
- residual: bfloat16 [256, 4096], P('ctx'), may hold values from -6 to 6
- gain: float32 [4096], replicated, may hold values from 0.1 to 1.9
- routes: int32 [256, 2], P('ctx'), may hold values from 0 to 7, all different within a row; in each aligned block of 8 rows (0 to 7, 8 to 15, ...) at most 4 rows name the same one
- gates: float32 [256, 2], P('ctx'), may hold values from 0.25 to 1
- w_gate: bfloat16 [8, 4096, 14336], P('exp', None, 'ctx'), may hold values from -0.09375 to 0.09375
- w_up: bfloat16 [8, 4096, 14336], P('exp', None, 'ctx'), may hold values from -0.09375 to 0.09375
- w_down: bfloat16 [8, 14336, 4096], P('exp', 'ctx'), may hold values from -0.046875 to 0.046875
Outputs:
- mixed: bfloat16 [256, 4096], P('ctx', 'exp')
Inputs may be any that keep to these rules, and one draw needn't show every extreme that they name: `routes`: within each aligned block of 8 rows no expert is named by more than 4 rows, some expert is named by exactly 4 rows in some block, and the 2 experts of a row differ.
All inputs are finite; a program needn't handle non-finite values.
Results may differ from a plain program's by a relative error of at most 0.017.
Values may be sent and summed in bfloat16 or wider, within the bound.
A program may use at most 128 MiB of HBM per device.

v0:
```python
import math
import jax
import jax.numpy as jnp
from jax import lax
from jax.sharding import PartitionSpec as P


def joined(part, axis, combine):
    gathered = jax.tree.map(lambda a: lax.all_gather(a, axis), part)

    def take(source):
        return jax.tree.map(lambda a: lax.dynamic_index_in_dim(a, source, 0, False), gathered)

    return lax.fori_loop(
        1, lax.axis_size(axis), lambda source, state: combine(state, take(source)), take(0)
    )


def combine_parts(first_part, second_part):
    top_level = jnp.maximum(first_part[0], second_part[0])
    first_scale = jnp.exp(first_part[0] - top_level)
    second_scale = jnp.exp(second_part[0] - top_level)
    summed = first_part[1] * first_scale + second_part[1] * second_scale
    weighted = first_part[2] * first_scale[..., None] + second_part[2] * second_scale[..., None]
    return (top_level, summed, weighted)


def local(queries, keys, values, out_proj, residual, gain, routes, gates, w_gate, w_up, w_down):
    tokens_all, heads_local, head_dim = queries.shape
    key_rows, kv_local, unused_dim = keys.shape
    groups = heads_local // kv_local
    ctx_count = lax.axis_size("ctx")
    ctx_index = lax.axis_index("ctx")
    exp_index = lax.axis_index("exp")
    block_rows = residual.shape[0]
    total_len = key_rows * ctx_count
    score_scale = 1.0 / math.sqrt(head_dim)
    grouped = queries.reshape(tokens_all, kv_local, groups, head_dim)
    scores = (
        jnp.einsum("tgrd,sgd->gtrs", grouped, keys, preferred_element_type=jnp.float32)
        * score_scale
    )
    key_pos = ctx_index * key_rows + jnp.arange(key_rows, dtype=jnp.int32)
    query_pos = total_len - tokens_all + jnp.arange(tokens_all, dtype=jnp.int32)
    visible = (key_pos[None, :] <= query_pos[:, None])[None, :, None, :]
    scores = jnp.where(visible, scores, jnp.float32(-1e30))
    block_max = jnp.max(scores, axis=-1)
    expw = jnp.where(visible, jnp.exp(scores - block_max[..., None]), jnp.float32(0.0))
    block_sum = jnp.sum(expw, axis=-1)
    block_out = jnp.einsum(
        "gtrs,sgd->gtrd", expw.astype(jnp.bfloat16), values, preferred_element_type=jnp.float32
    )
    merged = joined((block_max, block_sum, block_out), "ctx", combine_parts)
    attended_all = merged[2] / merged[1][..., None]
    own_rows = lax.dynamic_slice_in_dim(attended_all, ctx_index * block_rows, block_rows, 1)
    attended = (
        own_rows.transpose(1, 0, 2, 3)
        .reshape(block_rows, heads_local * head_dim)
        .astype(jnp.bfloat16)
    )
    partial_value = jnp.dot(
        attended,
        lax.all_gather(out_proj, "ctx", axis=1, tiled=True),
        preferred_element_type=jnp.float32,
    )
    stream = residual.astype(jnp.float32) + lax.psum(
        partial_value.astype(jnp.bfloat16), "exp"
    ).astype(jnp.float32)
    normed = (
        stream * lax.rsqrt(jnp.mean(stream * stream, axis=-1, keepdims=True) + 1e-05) * gain
    ).astype(jnp.bfloat16)
    experts_local = w_gate.shape[0]
    expert_count = experts_local * lax.axis_size("exp")
    top_count = routes.shape[1]
    capacity = min(block_rows, 2 * top_count * block_rows // expert_count)
    flat_ids = routes.reshape(block_rows * top_count)
    onehot = (flat_ids[:, None] == jnp.arange(expert_count, dtype=jnp.int32)[None, :]).astype(
        jnp.int32
    )
    before = jnp.cumsum(onehot, axis=0, dtype=jnp.int32) - onehot
    slot_of = jnp.sum(before * onehot, axis=1, dtype=jnp.int32)
    mine_ids = exp_index * experts_local + jnp.arange(experts_local, dtype=jnp.int32)
    is_mine = flat_ids[:, None] == mine_ids[None, :]
    slot_hit = is_mine[:, :, None] & (
        slot_of[:, None, None] == jnp.arange(capacity, dtype=jnp.int32)[None, None, :]
    )
    slot_hit = slot_hit.astype(jnp.float32).reshape(block_rows, top_count, experts_local, capacity)
    dispatch_map = jnp.sum(slot_hit, axis=1)
    combine_map = jnp.sum(slot_hit * gates[:, :, None, None], axis=1)
    buffer = jnp.einsum(
        "tec,td->ced", dispatch_map.astype(jnp.bfloat16), normed, preferred_element_type=jnp.float32
    ).astype(jnp.bfloat16)
    shard_rows = lax.all_gather(buffer, "ctx", axis=0, tiled=True)
    gate_val = jnp.einsum("ned,edf->nef", shard_rows, w_gate, preferred_element_type=jnp.float32)
    up_val = jnp.einsum("ned,edf->nef", shard_rows, w_up, preferred_element_type=jnp.float32)
    act = (jax.nn.silu(gate_val) * up_val).astype(jnp.bfloat16)
    expert_out = lax.psum_scatter(
        jnp.einsum("nef,efd->ned", act, w_down, preferred_element_type=jnp.float32).astype(
            jnp.bfloat16
        ),
        "ctx",
        scatter_dimension=0,
        tiled=True,
    ).astype(jnp.float32)
    contribution = jnp.einsum(
        "tec,ced->td", combine_map, expert_out, precision=lax.Precision.HIGHEST
    )
    moe_share = lax.psum_scatter(
        contribution.astype(jnp.bfloat16), "exp", scatter_dimension=1, tiled=True
    ).astype(jnp.float32)
    feat_width = moe_share.shape[1]
    own_stream = lax.dynamic_slice_in_dim(stream, exp_index * feat_width, feat_width, 1)
    return (own_stream + moe_share).astype(jnp.bfloat16)


def solution(mesh):
    return jax.shard_map(
        local,
        mesh=mesh,
        in_specs=(
            P(None, "exp", None),
            P("ctx", "exp", None),
            P("ctx", "exp", None),
            P("exp", "ctx"),
            P("ctx", None),
            P(),
            P("ctx", None),
            P("ctx", None),
            P("exp", None, "ctx"),
            P("exp", None, "ctx"),
            P("exp", "ctx", None),
        ),
        out_specs=P("ctx", "exp"),
        check_vma=False,
    )
```

profile of v0, /device:TPU:2, one launch (start us, length us, event | category | flops | bytes accessed | tf_op | source)
XLA Modules:
  0.0 1042.4 jit_solution(11815722336202214809)
XLA Ops:
  7.5 2.0 fusion.8
  9.5 2.0 copy-done.1
  11.4 2.2 fusion.16
  14.5 3.7 fusion.15
  18.1 112.5 %all-gather = f32[8192,4]{0,1:T(4,128)S(1)} all-gather(f32[256,4]{0,1:T(4,128)S(1)} %get-tuple-element.241), channel_id=2, replica_groups=mesh['ctx'=32,'exp'=8] {'ctx'}, dimensions={0}, use_global_device_ids=true | all-gather | bytes 135168 | tf_op jit(solution)/shard_map/all_gather | solution.py:9
  130.7 123.6 %all-gather.1 = f32[8192,4]{0,1:T(4,128)S(1)} all-gather(f32[256,4]{0,1:T(4,128)S(1)} %fusion.15), channel_id=3, replica_groups=mesh['ctx'=32,'exp'=8] {'ctx'}, dimensions={0}, use_global_device_ids=true | all-gather | bytes 135168 | tf_op jit(solution)/shard_map/all_gather | solution.py:9
  254.9 12.9 %all-gather.11.cloned.1.call-done = f32[8192,4,128]{2,0,1:T(8,128)} async-done(((f32[256,4,128]{2,0,1:T(8,128)}), f32[8192,4,128]{2,0,1:T(8,128)}) %all-gather.11.cloned.1.call-update) | async-done | bytes 16777232 | tf_op jit(solution)/shard_map/all_gather | solution.py:9
  269.3 84.7 %while.19 = (s32[]{:T(128)}, f32[1,256,4]{1,2,0:T(4,128)S(1)}, f32[1,256,4]{1,2,0:T(4,128)S(1)}, f32[1,256,4,128]{3,2,1,0:T(4,128)S(1)}, f32[32,1,256,4]{2,3,1,0...) while((s32[]{:T(128)}, f32[1,256,4]{1,2,0:T(4,128)S(1)}, ...), condition=%wide.region_3.4_spmd, body=%wide.region_2.3_spmd.sunk | while | flops 400389 | bytes 2699419 | solution.py:14
  269.7 1.1 constant_dynamic-slice_fusion.3
  270.8 1.3 fusion.75
  272.4 1.1 constant_dynamic-slice_fusion.3
  273.5 1.3 fusion.75
  276.2 1.3 fusion.75
  277.9 1.1 constant_dynamic-slice_fusion.3
  279.0 1.3 fusion.75
  281.7 1.3 fusion.75
  283.3 1.1 constant_dynamic-slice_fusion.3
  284.4 1.3 fusion.75
  287.2 1.3 fusion.75
  288.8 1.1 constant_dynamic-slice_fusion.3
  289.9 1.3 fusion.75
  291.5 1.1 constant_dynamic-slice_fusion.3
  292.6 1.3 fusion.75
  295.4 1.3 fusion.75
  297.0 1.1 constant_dynamic-slice_fusion.3
  298.1 1.3 fusion.75
  300.8 1.3 fusion.75
  303.5 1.3 fusion.75
  305.2 1.1 constant_dynamic-slice_fusion.3
  306.3 1.3 fusion.75
  307.9 1.1 constant_dynamic-slice_fusion.3
  309.0 1.3 fusion.75
  311.7 1.3 fusion.75
  313.4 1.1 constant_dynamic-slice_fusion.3
  314.5 1.3 fusion.75
  317.2 1.3 fusion.75
  319.9 1.3 fusion.75
  321.6 1.1 constant_dynamic-slice_fusion.3
  322.7 1.3 fusion.75
  325.4 1.3 fusion.75
  327.0 1.1 constant_dynamic-slice_fusion.3
  328.1 1.3 fusion.75
  329.8 1.1 constant_dynamic-slice_fusion.3
  330.9 1.3 fusion.75
  332.5 1.1 constant_dynamic-slice_fusion.3
  333.6 1.3 fusion.75
  335.3 1.1 constant_dynamic-slice_fusion.3
  336.4 1.3 fusion.75
  339.1 1.3 fusion.75
  341.8 1.3 fusion.75
  344.5 1.3 fusion.75
  347.3 1.3 fusion.75
  350.0 1.3 fusion.75
  352.7 1.3 fusion.75
  354.3 45.0 %all-gather.7.cloned.1.call-done = bf16[512,4096]{1,0:T(8,128)(2,1)} async-done(((bf16[512,128]{1,0:T(8,128)(2,1)}), bf16[512,4096]{1,0:T(8,128)(2,1)}) %all-gather.7.cloned.1.call-update) | async-done | bytes 4194320 | tf_op jit(solution)/shard_map/all_gather | solution.py:63
  399.3 3.5 convolution_convert_fusion.2
  402.9 65.4 %all-reduce.4.cloned.1.call-done = bf16[8,4096]{1,0:T(8,128)(2,1)} async-done(((bf16[8,4096]{1,0:T(8,128)(2,1)}), bf16[8,4096]{1,0:T(8,128)(2,1)}) %all-reduce.4.cloned.1.call-update) | async-done | bytes 65552 | tf_op jit(solution)/shard_map/psum | solution.py:66
  471.1 90.5 %all-gather.9.cloned.1.call-done = bf16[128,1,4096]{2,1,0:T(2,128)(2,1)} async-done(((bf16[4,1,4096]{2,1,0:T(2,128)(2,1)}), bf16[128,1,4096]{2,1,0:T(2,128)(2,1)}) %all-gather.9.cloned.1.call-update) | async-done | bytes 1048592 | tf_op jit(solution)/shard_map/all_gather | solution.py:93
  561.6 4.8 fusion.19
  566.4 7.3 fusion.6
  574.9 405.6 %all-reduce.6.cloned.1.call-done = bf16[128,1,4096]{2,0,1:T(8,128)(2,1)} async-done(((bf16[128,1,4096]{2,0,1:T(8,128)(2,1)}), bf16[128,1,4096]{2,0,1:T(8,128)(2,1)}) %all-reduce.6.cloned.1.call-update) | async-done | bytes 1048592
  980.5 1.7 convolution_convert_fusion.1
  982.3 52.0 %reduce-scatter.3.cloned.1.call-done = bf16[8,512]{1,0:T(8,128)(2,1)} async-done(((bf16[8,4096]{1,0:T(8,128)(2,1)}), bf16[8,512]{1,0:T(8,128)(2,1)}) %reduce-scatter.3.cloned.1.call-update) | async-done | bytes 8208 | tf_op jit(solution)/shard_map/reduce_scatter | solution.py:108
  1034.3 1.3 add_convert_fusion
  (224 shorter events, 34.6 us)
Async XLA Ops:
  6.5 1.0 copy-start
  6.5 4.9 copy-start.7
  6.5 261.3 %all-gather.11.cloned.1.call-start = ((), (), s32[]{:S(2)}) async-start(), calls=%async_computation.5 | async-start | bytes 17301504 | tf_op jit(solution)/shard_map/all_gather | solution.py:9
  9.4 2.0 copy-start.1
  13.6 240.7 %copy-start.5 = (s32[8,2]{0,1:T(2,128)S(1)}, s32[8,2]{0,1:T(2,128)}, u32[]{:S(2)}) copy-start(s32[8,2]{0,1:T(2,128)} %param.19) | copy-start | bytes 196
  13.7 385.6 %all-gather.7.cloned.1.call-start = ((), (), s32[]{:S(2)}) async-start(), calls=%async_computation.1 | async-start | bytes 4325376 | tf_op jit(solution)/shard_map/all_gather | solution.py:63
  14.4 453.8 %all-reduce.4.cloned.1.call-start = ((), (), s32[]{:S(2)}) async-start(), calls=%async_computation.2 | async-start | bytes 131072 | tf_op jit(solution)/shard_map/psum | solution.py:66
  354.0 48.8 %copy-start.6 = (f32[8,2]{0,1:T(2,128)S(1)}, f32[8,2]{0,1:T(2,128)}, u32[]{:S(2)}) copy-start(f32[8,2]{0,1:T(2,128)} %param.20) | copy-start | bytes 196
  354.0 114.2 %copy-start.3 = (bf16[8,4096]{1,0:T(8,128)(2,1)S(1)}, bf16[8,4096]{1,0:T(8,128)(2,1)}, u32[]{:S(2)}) copy-start(bf16[8,4096]{1,0:T(8,128)(2,1)} %param.17) | copy-start | bytes 196612
  354.1 115.2 %copy-start.4 = (f32[4096]{0:T(1024)S(1)}, f32[4096]{0:T(1024)}, u32[]{:S(2)}) copy-start(f32[4096]{0:T(1024)} %param.18) | copy-start | bytes 49156
  402.8 158.8 %all-gather.9.cloned.1.call-start = ((), (), s32[]{:S(2)}) async-start(), calls=%async_computation.3 | async-start | bytes 2162688 | tf_op jit(solution)/shard_map/all_gather | solution.py:93
  471.0 509.5 %all-reduce.6.cloned.1.call-start = ((), (), s32[]{:S(2)}) async-start(), calls=%async_computation.6 | async-start | bytes 2097152
  561.6 4.8 copy-start.2
  566.3 7.4 copy-start.8
  573.6 460.6 %reduce-scatter.3.cloned.1.call-start = ((), (), s32[]{:S(2)}) async-start(), calls=%async_computation.4 | async-start | bytes 73728 | tf_op jit(solution)/shard_map/reduce_scatter | solution.py:108
Sparse Core Ops, SparseCore 0:
  13.8 254.0 all-gather.10
  271.1 128.1 all-gather.6
  402.9 65.3 all-reduce.3
  472.2 89.3 all-gather.8
  573.8 406.6 all-reduce.5
  982.9 51.3 reduce-scatter.2
where the time goes:
time: 1040 us
  waiting for transfers between devices  672 us (65%)
  blocking collectives  236 us (23%)
  local copies, waits for them, and re-layouts  48.1 us (5%)
  other arithmetic  47.1 us (5%)
  matrix products  22.4 us (2%)
  between operations  14.3 us (1%)
    unnamed x7, waiting for transfers between devices  406 us
    all_gather x2, blocking collectives, joined(): gathered = jax.tree.map(lambda a: lax.all_gather(a, axis), part)  236 us
    all_gather x1, waiting for transfers between devices, local(): shard_rows = lax.all_gather(buffer, 'ctx', axis=0, tiled=True)  90.5 us
    psum x1, waiting for transfers between devices, local(): lax.psum(partial_value.astype(jnp.bfloat16), 'exp').astype(jnp.float32)  65.4 us
    reduce_scatter x1, waiting for transfers between devices, local(): lax.psum_scatter(contribution.astype(jnp.bfloat16), 'exp', scatter_dimens...  52 us
    all_gather x1, waiting for transfers between devices, local(): lax.all_gather(out_proj, 'ctx', axis=1, tiled=True)  45 us
    add x31, other arithmetic, combine_parts(): first_part[2] * first_scale[..., None]  39.3 us
    dynamic_slice x31, local copies, waits for them, and re-layouts, take(): lax.dynamic_index_in_dim(a, source, 0, False)  33.8 us
  transfers between devices with their start and end apart: 6, of which 6 were waited for; matrix products, arithmetic and copies ran while one was open for 9% of the time, Pallas kernels for 0%

commit v1 on v0

--- a/solution.py
+++ b/solution.py
@@ -58,10 +58,20 @@
         .reshape(block_rows, heads_local * head_dim)
         .astype(jnp.bfloat16)
     )
+
+    def link_sector(local_array, row_axis):
+        return jnp.concatenate(
+            lax.all_to_all(
+                jnp.stack([local_array for _ in range(lax.psum(1, row_axis))], axis=0),
+                axis_name=row_axis,
+                split_axis=0,
+                concat_axis=0,
+            ),
+            axis=1,
+        )
+
     partial_value = jnp.dot(
-        attended,
-        lax.all_gather(out_proj, "ctx", axis=1, tiled=True),
-        preferred_element_type=jnp.float32,
+        attended, link_sector(out_proj, "ctx"), preferred_element_type=jnp.float32
     )
     stream = residual.astype(jnp.float32) + lax.psum(
         partial_value.astype(jnp.bfloat16), "exp"

time: 1040 us -> 1120 us (1.077)
  blocking collectives: 236 us -> 328 us
  waiting for transfers between devices: 672 us -> 636 us
  starting transfers between devices: 0.21 us -> 14.8 us
    all_gather x2, blocking collectives: 236 us -> 328 us  [joined(): gathered = jax.tree.map(lambda a: lax.all_gather(a, axis), part)]
    all_gather x1 -> x0, waiting for transfers between devices: 45 us -> none  [local(): lax.all_gather(out_proj, 'ctx', axis=1, tiled=True)]
    psum x1, waiting for transfers between devices: 65.4 us -> 88.1 us  [local(): lax.psum(partial_value.astype(jnp.bfloat16), 'exp').astype(jnp.float32)]
    all_to_all x0 -> x1, starting transfers between devices: none -> 14.4 us  [link_sector(): lax.all_to_all(jnp.stack([local_array for _ in range(lax.psum(1, row_axis...]
    all_gather x1, waiting for transfers between devices: 12.9 us -> 0.02 us  [joined(): gathered = jax.tree.map(lambda a: lax.all_gather(a, axis), part)]
    unnamed x7 -> x6, waiting for transfers between devices: 406 us -> 406 us
  transfers between devices with their start and end apart: 6 -> 6, of which waited for: 6 -> 4; matrix products, arithmetic and copies ran while one was open for 9% -> 8% of each run, Pallas kernels for 0% -> 0%
where the time goes in v1:
time: 1120 us
  waiting for transfers between devices  636 us (57%)
  blocking collectives  328 us (29%)
  local copies, waits for them, and re-layouts  50.6 us (5%)
  other arithmetic  47.1 us (4%)
  matrix products  22.9 us (2%)
  starting transfers between devices  14.8 us (1%)
  between operations  14 us (1%)
    unnamed x6, waiting for transfers between devices  406 us
    all_gather x2, blocking collectives, joined(): gathered = jax.tree.map(lambda a: lax.all_gather(a, axis), part)  328 us
    all_gather x1, waiting for transfers between devices, local(): shard_rows = lax.all_gather(buffer, 'ctx', axis=0, tiled=True)  90.5 us
    psum x1, waiting for transfers between devices, local(): lax.psum(partial_value.astype(jnp.bfloat16), 'exp').astype(jnp.float32)  88.1 us
    reduce_scatter x1, waiting for transfers between devices, local(): lax.psum_scatter(contribution.astype(jnp.bfloat16), 'exp', scatter_dimens...  52 us
    add x31, other arithmetic, combine_parts(): first_part[2] * first_scale[..., None]  39.3 us
    dynamic_slice x31, local copies, waits for them, and re-layouts, take(): lax.dynamic_index_in_dim(a, source, 0, False)  33.7 us
  transfers between devices with their start and end apart: 6, of which 4 were waited for; matrix products, arithmetic and copies ran while one was open for 8% of the time, Pallas kernels for 0%

profile of v1, /device:TPU:2, one launch (start us, length us, event | category | flops | bytes accessed | tf_op | source)
XLA Modules:
  0.0 1115.4 jit_solution(8581246615379384005)
XLA Ops:
  7.5 2.0 fusion.8
  9.5 1.9 copy-done.1
  11.4 2.2 fusion.16
  13.8 2.4 stack.2
  16.2 14.4 %all-to-all-start = ((bf16[32,512,128]{1,2,0:T(8,128)(2,1)}), bf16[32,512,128]{1,2,0:T(8,128)(2,1)}, u32[]{:S(2)}, u32[]{:S(2)}) async-start(bf16[32,512,128]{1,2,0:T(8,128)(2,1)} %stack.2), calls=%async_computation | async-start | bytes 8388608 | tf_op jit(solution)/shard_map/all_to_all | solution.py:64
  31.3 213.7 %all-gather = f32[8192,4]{0,1:T(4,128)S(1)} all-gather(f32[256,4]{0,1:T(4,128)S(1)} %get-tuple-element.241), channel_id=2, replica_groups=mesh['ctx'=32,'exp'=8] {'ctx'}, dimensions={0}, use_global_device_ids=true | all-gather | bytes 135168 | tf_op jit(solution)/shard_map/all_gather | solution.py:9
  245.0 3.7 fusion.15
  248.7 113.9 %all-gather.1 = f32[8192,4]{0,1:T(4,128)S(1)} all-gather(f32[256,4]{0,1:T(4,128)S(1)} %fusion.15), channel_id=3, replica_groups=mesh['ctx'=32,'exp'=8] {'ctx'}, dimensions={0}, use_global_device_ids=true | all-gather | bytes 135168 | tf_op jit(solution)/shard_map/all_gather | solution.py:9
  364.1 84.7 %while.19 = (s32[]{:T(128)}, f32[1,256,4]{1,2,0:T(4,128)S(1)}, f32[1,256,4]{1,2,0:T(4,128)S(1)}, f32[1,256,4,128]{3,2,1,0:T(4,128)S(1)}, f32[32,1,256,4]{2,3,1,0...) while((s32[]{:T(128)}, f32[1,256,4]{1,2,0:T(4,128)S(1)}, ...), condition=%wide.region_3.4_spmd, body=%wide.region_2.3_spmd.sunk | while | flops 400389 | bytes 2699419 | solution.py:14
  364.5 1.1 constant_dynamic-slice_fusion.3
  365.5 1.3 fusion.75
  367.2 1.1 constant_dynamic-slice_fusion.3
  368.3 1.3 fusion.75
  369.9 1.1 constant_dynamic-slice_fusion.3
  371.0 1.3 fusion.75
  372.6 1.1 constant_dynamic-slice_fusion.3
  373.7 1.3 fusion.75
  375.4 1.1 constant_dynamic-slice_fusion.3
  376.5 1.3 fusion.75
  379.2 1.3 fusion.75
  381.9 1.3 fusion.75
  383.6 1.1 constant_dynamic-slice_fusion.3
  384.7 1.3 fusion.75
  387.4 1.3 fusion.75
  390.1 1.3 fusion.75
  391.8 1.1 constant_dynamic-slice_fusion.3
  392.9 1.3 fusion.75
  395.6 1.3 fusion.75
  397.2 1.1 constant_dynamic-slice_fusion.3
  398.3 1.3 fusion.75
  400.0 1.1 constant_dynamic-slice_fusion.3
  401.0 1.3 fusion.75
  403.8 1.3 fusion.75
  405.4 1.1 constant_dynamic-slice_fusion.3
  406.5 1.3 fusion.75
  409.2 1.3 fusion.75
  412.0 1.3 fusion.75
  413.6 1.1 constant_dynamic-slice_fusion.3
  414.7 1.3 fusion.75
  417.4 1.3 fusion.75
  420.2 1.3 fusion.75
  421.8 1.1 constant_dynamic-slice_fusion.3
  422.9 1.3 fusion.75
  425.6 1.3 fusion.75
  427.3 1.1 constant_dynamic-slice_fusion.3
  428.4 1.3 fusion.75
  431.1 1.3 fusion.75
  433.8 1.3 fusion.75
  435.5 1.1 constant_dynamic-slice_fusion.3
  436.6 1.3 fusion.75
  439.3 1.3 fusion.75
  442.0 1.3 fusion.75
  443.7 1.1 constant_dynamic-slice_fusion.3
  444.7 1.3 fusion.75
  447.5 1.3 fusion.75
  449.1 4.0 convolution_convert_fusion.2
  453.2 88.1 %all-reduce.4.cloned.1.call-done = bf16[8,4096]{1,0:T(8,128)(2,1)} async-done(((bf16[8,4096]{1,0:T(8,128)(2,1)}), bf16[8,4096]{1,0:T(8,128)(2,1)}) %all-reduce.4.cloned.1.call-update) | async-done | bytes 65552 | tf_op jit(solution)/shard_map/psum | solution.py:76
  544.2 90.5 %all-gather.6.cloned.1.call-done = bf16[128,1,4096]{2,1,0:T(2,128)(2,1)} async-done(((bf16[4,1,4096]{2,1,0:T(2,128)(2,1)}), bf16[128,1,4096]{2,1,0:T(2,128)(2,1)}) %all-gather.6.cloned.1.call-update) | async-done | bytes 1048592 | tf_op jit(solution)/shard_map/all_gather | solution.py:103
  634.7 4.8 fusion.19
  639.5 7.3 fusion.6
  648.1 405.7 %all-reduce.6.cloned.1.call-done = bf16[128,1,4096]{2,0,1:T(8,128)(2,1)} async-done(((bf16[128,1,4096]{2,0,1:T(8,128)(2,1)}), bf16[128,1,4096]{2,0,1:T(8,128)(2,1)}) %all-reduce.6.cloned.1.call-update) | async-done | bytes 1048592
  1053.8 1.7 convolution_convert_fusion.1
  1055.5 52.0 %reduce-scatter.3.cloned.1.call-done = bf16[8,512]{1,0:T(8,128)(2,1)} async-done(((bf16[8,4096]{1,0:T(8,128)(2,1)}), bf16[8,512]{1,0:T(8,128)(2,1)}) %reduce-scatter.3.cloned.1.call-update) | async-done | bytes 8208 | tf_op jit(solution)/shard_map/reduce_scatter | solution.py:118
  1107.5 1.3 add_convert_fusion
  (227 shorter events, 34.2 us)
Async XLA Ops:
  6.5 1.0 copy-start
  6.5 4.9 copy-start.8
  6.5 356.1 %all-gather.8.cloned.1.call-start = ((), (), s32[]{:S(2)}) async-start(), calls=%async_computation.5 | async-start | bytes 17301504 | tf_op jit(solution)/shard_map/all_gather | solution.py:9
  9.4 2.0 copy-start.1
  11.4 2.2 copy-start.4
  16.2 14.5 %copy-start.6 = (s32[8,2]{0,1:T(2,128)S(1)}, s32[8,2]{0,1:T(2,128)}, u32[]{:S(2)}) copy-start(s32[8,2]{0,1:T(2,128)} %param.19) | copy-start | bytes 196
  16.2 432.9 %all-to-all-start = ((bf16[32,512,128]{1,2,0:T(8,128)(2,1)}), bf16[32,512,128]{1,2,0:T(8,128)(2,1)}, u32[]{:S(2)}, u32[]{:S(2)}) async-start(bf16[32,512,128]{1,2,0:T(8,128)(2,1)} %stack.2), calls=%async_computation | async-start | bytes 8388608 | tf_op jit(solution)/shard_map/all_to_all | solution.py:64
  30.6 510.6 %all-reduce.4.cloned.1.call-start = ((), (), s32[]{:S(2)}) async-start(), calls=%async_computation.2 | async-start | bytes 131072 | tf_op jit(solution)/shard_map/psum | solution.py:76
  448.8 4.4 copy-start.7
  448.8 92.5 %copy-start.3 = (bf16[8,4096]{1,0:T(8,128)(2,1)S(1)}, bf16[8,4096]{1,0:T(8,128)(2,1)}, u32[]{:S(2)}) copy-start(bf16[8,4096]{1,0:T(8,128)(2,1)} %param.17) | copy-start | bytes 196612
  448.8 93.5 %copy-start.5 = (f32[4096]{0:T(1024)S(1)}, f32[4096]{0:T(1024)}, u32[]{:S(2)}) copy-start(f32[4096]{0:T(1024)} %param.18) | copy-start | bytes 49156
  453.1 181.6 %all-gather.6.cloned.1.call-start = ((), (), s32[]{:S(2)}) async-start(), calls=%async_computation.3 | async-start | bytes 2162688 | tf_op jit(solution)/shard_map/all_gather | solution.py:103
  544.0 509.8 %all-reduce.6.cloned.1.call-start = ((), (), s32[]{:S(2)}) async-start(), calls=%async_computation.6 | async-start | bytes 2097152
  634.7 4.8 copy-start.2
  639.5 7.4 copy-start.9
  646.8 460.8 %reduce-scatter.3.cloned.1.call-start = ((), (), s32[]{:S(2)}) async-start(), calls=%async_computation.4 | async-start | bytes 73728 | tf_op jit(solution)/shard_map/reduce_scatter | solution.py:118
Sparse Core Ops, SparseCore 0:
  13.7 327.7 all-gather.7
  453.2 87.9 all-reduce.3
  545.3 89.3 all-gather.5
  646.9 406.8 all-reduce.5
  1056.1 51.3 reduce-scatter.2
